TPU v7x, 256 devices: a whole 4x4x8 slice. The times are simulated.
256 devices in a mesh: dp: 16 (over z, core), mp: 16 (over y, x).
Axes of the slice: x: 4, y: 4, z: 8, core: 2. Of those that a mesh axis runs over, the one named last changes fastest.
Arguments:
- candidates: bfloat16 [4096, 4096], P('dp', 'mp'), may hold values from -6 to 6
- hold_gate: bfloat16 [4096, 8192], P(None, 'mp'), may hold values from -0.09375 to 0.09375
- hold_up: bfloat16 [4096, 8192], P(None, 'mp'), may hold values from -0.09375 to 0.09375
- probe: float32 [8192], P('mp'), as said below
- chosen: int32 [16, 192], replicated, may hold values from 0 to 4095, as said below
- counts: int32 [16], replicated, may hold values from 24 to 192, as said below
- gate_w: bfloat16 [4096, 14336], P('dp', 'mp'), may hold values from -0.09375 to 0.09375
- up_w: bfloat16 [4096, 14336], P('dp', 'mp'), may hold values from -0.09375 to 0.09375
- cotangent: bfloat16 [3072, 14336], P('dp', 'mp'), may hold values from -6 to 6
Outputs:
- grad_gate: bfloat16 [4096, 14336], P('dp', 'mp')
- grad_up: bfloat16 [4096, 14336], P('dp', 'mp')
- hidden: bfloat16 [3072, 14336], P('dp', 'mp')
- cand_weight: float32 [4096], P('dp')
Inputs may be any that keep to these rules, and one draw needn't show every extreme that they name: `chosen`: all entries are distinct candidate indices. `counts`: exactly one training shard uses all 192 slots in every draw. `probe`: magnitudes at most 12 / sqrt(8192).
All inputs are finite; a program needn't handle non-finite values.
Results may differ from a plain program's by a relative error of at most 0.0057.
Values may be sent and summed in bfloat16 or wider, within the bound.
A program may use at most 128 MiB of HBM per device.

v0:
```python
import jax
import jax.numpy as jnp
from jax import lax
from jax.sharding import PartitionSpec as P


def gather_by_a2a(x, axis_name, axis):
    parts = lax.psum(1, axis_name)
    stacked = lax.all_to_all(
        jnp.broadcast_to(x[None], (parts,) + x.shape),
        axis_name,
        split_axis=0,
        concat_axis=0,
        tiled=True,
    )
    stacked = jnp.moveaxis(stacked, 0, axis)
    shape = list(x.shape)
    shape[axis] *= parts
    return stacked.reshape(shape)


def on_device(candidates, hold_gate, hold_up, probe, chosen, counts, gate_w, up_w, cotangent):
    cand_dev = candidates.shape[0]
    shards = chosen.shape[0]
    slots = chosen.shape[1]
    width = candidates.shape[1]
    ff = gate_w.shape[1]
    merged = lax.all_gather(jnp.concatenate([candidates, gate_w], axis=1), "dp", axis=0, tiled=True)
    all_cands = merged[:, :width]
    full_w = (merged[:, width:], lax.all_gather(up_w, "dp", axis=0, tiled=True))
    own_index = lax.axis_index("dp")
    source = chosen // cand_dev
    local_row = (chosen % cand_dev).reshape(-1)
    valid = jnp.arange(slots, dtype=jnp.int32)[None, :] < counts[:, None]
    usable = (valid & (source == own_index)).reshape(-1)
    onehot = (
        (local_row[:, None] == jnp.arange(cand_dev, dtype=jnp.int32)[None, :]) & usable[:, None]
    ).astype(jnp.bfloat16)
    own_chosen = lax.dynamic_index_in_dim(chosen, own_index, 0, keepdims=False)
    own_valid = lax.dynamic_index_in_dim(valid, own_index, 0, keepdims=False)
    own_onehot = (
        (own_chosen[:, None] == jnp.arange(all_cands.shape[0], dtype=jnp.int32)[None, :])
        & own_valid[:, None]
    ).astype(jnp.bfloat16)
    row_slab = jnp.dot(own_onehot, all_cands, preferred_element_type=jnp.float32).astype(
        jnp.bfloat16
    )
    row_x = gather_by_a2a(row_slab, "mp", 1)
    parts = lax.psum(1, "dp")
    row_blocks = row_x.reshape(row_x.shape[0], parts, -1).transpose(1, 0, 2)
    row_slices = lax.all_to_all(row_blocks, "dp", split_axis=0, concat_axis=0, tiled=True)
    row_slices = row_slices.reshape(-1, row_blocks.shape[2])
    incoming = gather_by_a2a(candidates, "mp", 1)
    hold_g = jnp.dot(incoming, hold_gate, preferred_element_type=jnp.float32)
    hold_u = jnp.dot(incoming, hold_up, preferred_element_type=jnp.float32)
    partial_score = jnp.sum(jax.nn.silu(hold_g) * hold_u * probe[None, :], axis=1)
    score = jnp.sum(gather_by_a2a(partial_score[None, :], "mp", 0), axis=0)
    cand_weight = jax.nn.sigmoid(score)
    picked_weight = (
        jnp.dot(
            onehot, cand_weight.astype(jnp.bfloat16)[:, None], preferred_element_type=jnp.float32
        )
        .astype(jnp.bfloat16)
        .reshape(shards, slots)
    )
    arrived_weight = lax.all_to_all(picked_weight, "dp", split_axis=0, concat_axis=0, tiled=True)
    row_weight = jnp.sum(arrived_weight.astype(jnp.float32), axis=0)
    gate = jnp.dot(row_x, full_w[0], preferred_element_type=jnp.float32)
    up = jnp.dot(row_x, full_w[1], preferred_element_type=jnp.float32)
    hidden = (jax.nn.silu(gate) * up).astype(jnp.bfloat16)
    back = cotangent.astype(jnp.float32) * row_weight[:, None]
    sig = jax.nn.sigmoid(gate)
    d_up = (back * gate * sig).astype(jnp.bfloat16)
    d_gate = (back * up * sig * (1.0 + gate * (1.0 - sig))).astype(jnp.bfloat16)
    contract_rows = (((0,), (0,)), ((), ()))
    d_both, row_slices = lax.optimization_barrier(
        (jnp.concatenate([d_gate, d_up], axis=1), row_slices)
    )
    both_d = lax.all_gather(d_both, "dp", axis=0, tiled=True)
    grads = lax.dot_general(
        row_slices, both_d, contract_rows, preferred_element_type=jnp.float32
    ).astype(jnp.bfloat16)
    return (grads[:, :ff], grads[:, ff:], hidden, cand_weight)


def solution(mesh):
    placed = (
        P("dp", "mp"),
        P(None, "mp"),
        P(None, "mp"),
        P("mp"),
        P(),
        P(),
        P("dp", "mp"),
        P("dp", "mp"),
        P("dp", "mp"),
    )
    return jax.shard_map(
        on_device,
        mesh=mesh,
        in_specs=placed,
        out_specs=(P("dp", "mp"), P("dp", "mp"), P("dp", "mp"), P("dp")),
        check_vma=False,
    )
```

profile of v0, /device:TPU:1, one launch (start us, length us, event | category | flops | bytes accessed | tf_op | source)
XLA Modules:
  0.0 239.8 jit_solution(12118811220462123746)
XLA Ops:
  7.2 1.9 pad_maximum_fusion.1
  10.1 1.5 broadcast_in_dim.6
  11.6 7.7 %all-to-all-start = ((bf16[16,256,256]{1,2,0:T(8,128)(2,1)}), bf16[16,256,256]{1,2,0:T(8,128)(2,1)S(1)}, u32[]{:S(2)}, u32[]{:S(2)}) async-start(bf16[16,256,256]{1,2,0:T(8,128)(2,1)} %broadcast_in_dim.6), calls=%async_computation | async-start | bytes 4194304 | tf_op jit(solution)/shard_map/all_to_all | solution.py:9
  19.4 30.8 %all-to-all-done = bf16[16,256,256]{1,2,0:T(8,128)(2,1)S(1)} async-done(((bf16[16,256,256]{1,2,0:T(8,128)(2,1)}), bf16[16,256,256]{1,2,0:T(8,128)(2,1)S(1)}, u32[]{:S(2)}, u32[]{:S(2)}) %all-to-all-start) | async-done | bytes 2097184 | tf_op jit(solution)/shard_map/all_to_all | solution.py:9
  50.3 3.7 %fusion.26 = f32[256,512]{1,0:T(8,128)S(1)} fusion(bf16[256,4096]{0,1:T(8,128)(2,1)S(1)} %bitcast.20, bf16[4096,512]{1,0:T(8,128)(2,1)} %param.10), kind=kOutput, calls=%fused_computation.42 | convolution fusion | flops 1073741824 | bytes 6815744 | tf_op jit(solution)/shard_map/dot_general | solution.py:54
  54.0 1.4 fusion.14
  56.0 3.9 %all-to-all-start.1 = ((f32[16,1,256]{2,1,0:T(1,128)}), f32[16,1,256]{2,1,0:T(1,128)S(1)}, u32[]{:S(2)}, u32[]{:S(2)}) async-start(f32[16,1,256]{2,1,0:T(1,128)} %broadcast_in_dim.7), calls=%async_computation.1 | async-start | bytes 32768 | tf_op jit(solution)/shard_map/all_to_all | solution.py:9
  60.1 6.2 %all-to-all-done.1 = f32[16,1,256]{2,1,0:T(1,128)S(1)} async-done(((f32[16,1,256]{2,1,0:T(1,128)}), f32[16,1,256]{2,1,0:T(1,128)S(1)}, u32[]{:S(2)}, u32[]{:S(2)}) %all-to-all-start.1) | async-done | bytes 16416 | tf_op jit(solution)/shard_map/all_to_all | solution.py:9
  66.9 2.5 %fusion.6 = f32[1,3072]{1,0:T(1,128)S(1)} fusion(bf16[256,1]{0,1:T(2,128)(2,1)S(1)} %reshape.45, s32[3072]{0:T(1024)S(1)} %eq.38, pred[3072]{0:T(1024)(128)(4,1)S(1)} %and.37), kind=kOutput, calls=%fused_computation.7 | convolution fusion | flops 3145728 | bytes 28160 | tf_op jit(solution)/shard_map/dot_general | solution.py:60
  69.4 0.7 all_to_all.24
  70.1 11.0 %all-to-all-start.2 = ((bf16[16,1,192]{2,1,0:T(2,128)(2,1)}), bf16[16,1,192]{2,1,0:T(2,128)(2,1)S(1)}, u32[]{:S(2)}, u32[]{:S(2)}) async-start(bf16[16,1,192]{2,1,0:T(2,128)(2,1)} %all_to_all.24), calls=%async_computation.2 | async-start | bytes 32768 | tf_op jit(solution)/shard_map/all_to_all | solution.py:66
  81.2 2.4 fusion.15
  83.5 4.9 %all-to-all-done.2 = bf16[16,1,192]{2,1,0:T(2,128)(2,1)S(1)} async-done(((bf16[16,1,192]{2,1,0:T(2,128)(2,1)}), bf16[16,1,192]{2,1,0:T(2,128)(2,1)S(1)}, u32[]{:S(2)}, u32[]{:S(2)}) %all-to-all-start.2) | async-done | bytes 6176 | tf_op jit(solution)/shard_map/all_to_all | solution.py:66
  88.6 25.6 %all_to_all.30 = bf16[16,192,256]{2,1,0:T(8,128)(2,1)} all-to-all(bf16[16,192,256]{2,1,0:T(8,128)(2,1)S(1)} %broadcast_in_dim.8), channel_id=1, replica_groups=mesh['dp'=16,'mp'=16] {'mp'}, dimensions={0} | all-to-all | bytes 3145728 | tf_op jit(solution)/shard_map/all_to_all | solution.py:9
  114.2 5.0 %all-to-all-start.4 = ((bf16[16,192,256]{2,1,0:T(8,128)(2,1)}), bf16[16,192,256]{2,1,0:T(8,128)(2,1)S(1)}, u32[]{:S(2)}, u32[]{:S(2)}) async-start(bf16[16,192,256]{2,1,0:T(8,128)(2,1)} %all_to_all.30), calls=%async_computation.4 | async-start | bytes 3145728 | tf_op jit(solution)/shard_map/all_to_all | solution.py:51
  119.3 1.6 copy.27
  121.0 5.9 %fusion = f32[192,896]{1,0:T(8,128)} fusion(bf16[192,4096]{1,0:T(8,128)(2,1)S(1)} %bitcast.22, bf16[4096,1152]{1,0:T(8,128)(2,1)} %all-gather.4.cloned.1.call-done), kind=kOutput, calls=%fused_computation | convolution fusion | flops 1409286144 | bytes 9601024 | tf_op jit(solution)/shard_map/dot_general | solution.py:68
  126.9 1.1 all-gather.6.cloned.1.call-done
  128.0 5.9 %multiply_convert_fusion = (bf16[192,896]{1,0:T(8,128)(2,1)}, bf16[192,896]{1,0:T(8,128)(2,1)S(1)}, bf16[192,896]{1,0:T(8,128)(2,1)S(1)}) fusion(f32[192,896]{1,0:T(8,128)} %fusion, f32[192]{0:T(256)S(1)} %convert_reduce_fusion, bf16[192,896]{1,0:T(8,128)(2,1)S(1)} %copy-done.4, bf16[192,4096]{1,0:T(8,128)(2,1)S(1)} %bitcast.23, ...), kind=kOutput, calls=%fused_computation.19 | convolution fusion | flops 1412382720 | bytes 10978048 | tf_op jit(solution)/shard_map/dot_general | solution.py:69
  133.9 0.9 pad_maximum_fusion
  134.8 23.4 %all-to-all-done.4 = bf16[16,192,256]{2,1,0:T(8,128)(2,1)S(1)} async-done(((bf16[16,192,256]{2,1,0:T(8,128)(2,1)}), bf16[16,192,256]{2,1,0:T(8,128)(2,1)S(1)}, u32[]{:S(2)}, u32[]{:S(2)}) %all-to-all-start.4) | async-done | bytes 1572896 | tf_op jit(solution)/shard_map/all_to_all | solution.py:51
  158.3 66.9 %all-gather.8.cloned.1.call-done = bf16[3072,1792]{1,0:T(8,128)(2,1)} async-done(((bf16[192,1792]{1,0:T(8,128)(2,1)}), bf16[3072,1792]{1,0:T(8,128)(2,1)}) %all-gather.8.cloned.1.call-update) | async-done | bytes 11010064 | tf_op jit(solution)/shard_map/all_gather | solution.py:79
  225.1 7.2 %convolution_convert_fusion = bf16[256,1792]{1,0:T(8,128)(2,1)S(1)} fusion(bf16[3072,256]{1,0:T(8,128)(2,1)S(1)} %bitcast.19, bf16[3072,1792]{1,0:T(8,128)(2,1)} %all-gather.8.cloned.1.call-done), kind=kOutput, calls=%fused_computation.8 | convolution fusion | flops 2819031040 | bytes 13500416 | tf_op jit(solution)/shard_map/dot_general | solution.py:80
  232.3 1.0 fusion.25
  (33 shorter events, 2.7 us)
Async XLA Ops:
  7.2 2.8 %copy-start = (bf16[256,256]{1,0:T(8,128)(2,1)S(1)}, bf16[256,256]{1,0:T(8,128)(2,1)}, u32[]{:S(2)}) copy-start(bf16[256,256]{1,0:T(8,128)(2,1)} %param.9) | copy-start | bytes 393220
  7.2 74.0 %all-gather.4.cloned.1.call-start = ((), (), s32[]{:S(2)}) async-start(), calls=%async_computation.5 | async-start | bytes 10027008 | tf_op jit(solution)/shard_map/all_gather | solution.py:28
  9.2 118.8 %all-gather.6.cloned.1.call-start = ((), (), s32[]{:S(2)}) async-start(), calls=%async_computation.6 | async-start | bytes 7798784 | tf_op jit(solution)/shard_map/all_gather | solution.py:30
  11.6 7.7 %copy-start.1 = (s32[16,192]{1,0:T(8,128)S(1)}, s32[16,192]{1,0:T(8,128)}, u32[]{:S(2)}) copy-start(s32[16,192]{1,0:T(8,128)} %param.13) | copy-start | bytes 36868
  11.6 7.7 %copy-start.2 = (s32[16]{0:T(128)S(1)}, s32[16]{0:T(128)}, u32[]{:S(2)}) copy-start(s32[16]{0:T(128)} %param.14) | copy-start | bytes 196
  11.6 38.7 %all-to-all-start = ((bf16[16,256,256]{1,2,0:T(8,128)(2,1)}), bf16[16,256,256]{1,2,0:T(8,128)(2,1)S(1)}, u32[]{:S(2)}, u32[]{:S(2)}) async-start(bf16[16,256,256]{1,2,0:T(8,128)(2,1)} %broadcast_in_dim.6), calls=%async_computation | async-start | bytes 4194304 | tf_op jit(solution)/shard_map/all_to_all | solution.py:9
  50.3 3.7 %copy-start.3 = (bf16[4096,512]{1,0:T(8,128)(2,1)S(1)}, bf16[4096,512]{1,0:T(8,128)(2,1)}, u32[]{:S(2)}) copy-start(bf16[4096,512]{1,0:T(8,128)(2,1)} %param.11) | copy-start | bytes 12582916
  50.3 3.7 %copy-start.5 = (f32[512]{0:T(512)S(1)}, f32[512]{0:T(512)}, u32[]{:S(2)}) copy-start(f32[512]{0:T(512)} %param.12) | copy-start | bytes 6148
  56.0 10.3 %all-to-all-start.1 = ((f32[16,1,256]{2,1,0:T(1,128)}), f32[16,1,256]{2,1,0:T(1,128)S(1)}, u32[]{:S(2)}, u32[]{:S(2)}) async-start(f32[16,1,256]{2,1,0:T(1,128)} %broadcast_in_dim.7), calls=%async_computation.1 | async-start | bytes 32768 | tf_op jit(solution)/shard_map/all_to_all | solution.py:9
  70.1 18.3 %all-to-all-start.2 = ((bf16[16,1,192]{2,1,0:T(2,128)(2,1)}), bf16[16,1,192]{2,1,0:T(2,128)(2,1)S(1)}, u32[]{:S(2)}, u32[]{:S(2)}) async-start(bf16[16,1,192]{2,1,0:T(2,128)(2,1)} %all_to_all.24), calls=%async_computation.2 | async-start | bytes 32768 | tf_op jit(solution)/shard_map/all_to_all | solution.py:66
  114.2 44.0 %all-to-all-start.4 = ((bf16[16,192,256]{2,1,0:T(8,128)(2,1)}), bf16[16,192,256]{2,1,0:T(8,128)(2,1)S(1)}, u32[]{:S(2)}, u32[]{:S(2)}) async-start(bf16[16,192,256]{2,1,0:T(8,128)(2,1)} %all_to_all.30), calls=%async_computation.4 | async-start | bytes 3145728 | tf_op jit(solution)/shard_map/all_to_all | solution.py:51
  119.3 105.9 %all-gather.8.cloned.1.call-start = ((), (), s32[]{:S(2)}) async-start(), calls=%async_computation.7 | async-start | bytes 11698176 | tf_op jit(solution)/shard_map/all_gather | solution.py:79
  121.0 7.0 %copy-start.4 = (bf16[192,896]{1,0:T(8,128)(2,1)S(1)}, bf16[192,896]{1,0:T(8,128)(2,1)}, u32[]{:S(2)}) copy-start(bf16[192,896]{1,0:T(8,128)(2,1)} %param.17) | copy-start | bytes 1032196
Sparse Core Ops, SparseCore 0:
  9.8 64.9 all-gather.3
  76.7 51.3 all-gather.5
  158.4 66.7 all-gather.7
where the time goes:
time: 240 us
  waiting for transfers between devices  134 us (56%)
  matrix products  28.9 us (12%)
  starting transfers between devices  27.7 us (12%)
  blocking collectives  25.6 us (11%)
  between operations  13.9 us (6%)
  local copies, waits for them, and re-layouts  5.97 us (2%)
  other arithmetic  3.59 us (1%)
    all_gather x1, waiting for transfers between devices, on_device(): both_d = lax.all_gather(d_both, 'dp', axis=0, tiled=True)  66.9 us
    all_to_all x2, waiting for transfers between devices, gather_by_a2a(): lax.all_to_all(jnp.broadcast_to(x[None], (parts,) + x.shape), axis_name,...  37.1 us
    all_to_all x1, blocking collectives, gather_by_a2a(): lax.all_to_all(jnp.broadcast_to(x[None], (parts,) + x.shape), axis_name,...  25.6 us
    all_to_all x1, waiting for transfers between devices, on_device(): lax.all_to_all(row_blocks, 'dp', split_axis=0, concat_axis=0, tiled=True)  23.4 us
    all_to_all x2, starting transfers between devices, gather_by_a2a(): lax.all_to_all(jnp.broadcast_to(x[None], (parts,) + x.shape), axis_name,...  11.6 us
    all_to_all x1, starting transfers between devices, on_device(): lax.all_to_all(picked_weight, 'dp', split_axis=0, concat_axis=0, tiled=True)  11 us
    dot_general x1, matrix products, on_device(): lax.dot_general(row_slices, both_d, contract_rows, preferred_element_type...  7.17 us
    dot_general x1, matrix products, on_device(): up = jnp.dot(row_x, full_w[1], preferred_element_type=jnp.float32)  5.92 us
  transfers between devices with their start and end apart: 7, of which 6 were waited for; matrix products, arithmetic and copies ran while one was open for 12% of the time, Pallas kernels for 0%

commit v1 on v0

--- a/solution.py
+++ b/solution.py
@@ -76,7 +76,9 @@
     d_both, row_slices = lax.optimization_barrier(
         (jnp.concatenate([d_gate, d_up], axis=1), row_slices)
     )
-    both_d = lax.all_gather(d_both, "dp", axis=0, tiled=True)
+    both_d = jnp.concatenate(
+        lax.all_to_all(jnp.stack([d_both] * lax.axis_size("dp")), "dp", 0, 0), axis=0
+    )
     grads = lax.dot_general(
         row_slices, both_d, contract_rows, preferred_element_type=jnp.float32
     ).astype(jnp.bfloat16)

time: 240 us -> 421 us (1.75)
  blocking collectives: 25.6 us -> 272 us
  waiting for transfers between devices: 134 us -> 68.1 us
  local copies, waits for them, and re-layouts: 5.97 us -> 11.2 us
    all_to_all x0 -> x1, blocking collectives: none -> 246 us  [on_device(): lax.all_to_all(jnp.stack([d_both] * lax.axis_size('dp')), 'dp', 0, 0)]
    all_gather x1 -> x0, waiting for transfers between devices: 66.9 us -> none  [on_device(): both_d = lax.all_gather(d_both, 'dp', axis=0, tiled=True)]
    another operation x0 -> x1, local copies, waits for them, and re-layouts: none -> 5.25 us  [on_device(): jnp.stack([d_both] * lax.axis_size('dp'))]
  transfers between devices with their start and end apart: 7 -> 6, of which waited for: 6 -> 5; matrix products, arithmetic and copies ran while one was open for 12% -> 6% of each run, Pallas kernels for 0% -> 0%
where the time goes in v1:
time: 421 us
  blocking collectives  272 us (65%)
  waiting for transfers between devices  68.1 us (16%)
  starting transfers between devices  27.7 us (7%)
  matrix products  24.8 us (6%)
  between operations  14.2 us (3%)
  local copies, waits for them, and re-layouts  11.2 us (3%)
    all_to_all x1, blocking collectives, on_device(): lax.all_to_all(jnp.stack([d_both] * lax.axis_size('dp')), 'dp', 0, 0)  246 us
    all_to_all x2, waiting for transfers between devices, gather_by_a2a(): lax.all_to_all(jnp.broadcast_to(x[None], (parts,) + x.shape), axis_name,...  37.1 us
    all_to_all x1, blocking collectives, gather_by_a2a(): lax.all_to_all(jnp.broadcast_to(x[None], (parts,) + x.shape), axis_name,...  25.6 us
    all_to_all x1, waiting for transfers between devices, on_device(): lax.all_to_all(row_blocks, 'dp', split_axis=0, concat_axis=0, tiled=True)  24.2 us
    all_to_all x2, starting transfers between devices, gather_by_a2a(): lax.all_to_all(jnp.broadcast_to(x[None], (parts,) + x.shape), axis_name,...  11.6 us
    all_to_all x1, starting transfers between devices, on_device(): lax.all_to_all(picked_weight, 'dp', split_axis=0, concat_axis=0, tiled=True)  11 us
  transfers between devices with their start and end apart: 6, of which 5 were waited for; matrix products, arithmetic and copies ran while one was open for 6% of the time, Pallas kernels for 0%

profile of v1, /device:TPU:1, one launch (start us, length us, event | category | flops | bytes accessed | tf_op | source)
XLA Modules:
  0.0 420.8 jit_solution(3784547371898635857)
XLA Ops:
  7.2 2.0 pad_maximum_fusion.1
  10.1 1.5 broadcast_in_dim.6
  11.6 7.7 %all-to-all-start = ((bf16[16,256,256]{1,2,0:T(8,128)(2,1)}), bf16[16,256,256]{1,2,0:T(8,128)(2,1)S(1)}, u32[]{:S(2)}, u32[]{:S(2)}) async-start(bf16[16,256,256]{1,2,0:T(8,128)(2,1)} %broadcast_in_dim.6), calls=%async_computation | async-start | bytes 4194304 | tf_op jit(solution)/shard_map/all_to_all | solution.py:9
  19.4 30.8 %all-to-all-done = bf16[16,256,256]{1,2,0:T(8,128)(2,1)S(1)} async-done(((bf16[16,256,256]{1,2,0:T(8,128)(2,1)}), bf16[16,256,256]{1,2,0:T(8,128)(2,1)S(1)}, u32[]{:S(2)}, u32[]{:S(2)}) %all-to-all-start) | async-done | bytes 2097184 | tf_op jit(solution)/shard_map/all_to_all | solution.py:9
  50.3 3.7 fusion.26
  54.0 1.4 fusion.14
  56.0 3.9 all-to-all-start.1
  60.1 6.2 %all-to-all-done.1 = f32[16,1,256]{2,1,0:T(1,128)S(1)} async-done(((f32[16,1,256]{2,1,0:T(1,128)}), f32[16,1,256]{2,1,0:T(1,128)S(1)}, u32[]{:S(2)}, u32[]{:S(2)}) %all-to-all-start.1) | async-done | bytes 16416 | tf_op jit(solution)/shard_map/all_to_all | solution.py:9
  66.9 2.5 fusion.6
  69.4 0.7 all_to_all.28
  70.1 11.0 %all-to-all-start.2 = ((bf16[16,1,192]{2,1,0:T(2,128)(2,1)}), bf16[16,1,192]{2,1,0:T(2,128)(2,1)S(1)}, u32[]{:S(2)}, u32[]{:S(2)}) async-start(bf16[16,1,192]{2,1,0:T(2,128)(2,1)} %all_to_all.28), calls=%async_computation.2 | async-start | bytes 32768 | tf_op jit(solution)/shard_map/all_to_all | solution.py:66
  81.2 2.4 fusion.15
  83.5 4.9 %all-to-all-done.2 = bf16[16,1,192]{2,1,0:T(2,128)(2,1)S(1)} async-done(((bf16[16,1,192]{2,1,0:T(2,128)(2,1)}), bf16[16,1,192]{2,1,0:T(2,128)(2,1)S(1)}, u32[]{:S(2)}, u32[]{:S(2)}) %all-to-all-start.2) | async-done | bytes 6176 | tf_op jit(solution)/shard_map/all_to_all | solution.py:66
  88.6 25.6 %all_to_all.35 = bf16[16,192,256]{2,1,0:T(8,128)(2,1)} all-to-all(bf16[16,192,256]{2,1,0:T(8,128)(2,1)S(1)} %broadcast_in_dim.8), channel_id=1, replica_groups=mesh['dp'=16,'mp'=16] {'mp'}, dimensions={0} | all-to-all | bytes 3145728 | tf_op jit(solution)/shard_map/all_to_all | solution.py:9
  114.2 5.0 %all-to-all-start.4 = ((bf16[16,192,256]{2,1,0:T(8,128)(2,1)}), bf16[16,192,256]{2,1,0:T(8,128)(2,1)S(1)}, u32[]{:S(2)}, u32[]{:S(2)}) async-start(bf16[16,192,256]{2,1,0:T(8,128)(2,1)} %all_to_all.35), calls=%async_computation.4 | async-start | bytes 3145728 | tf_op jit(solution)/shard_map/all_to_all | solution.py:51
  119.3 1.6 copy.27
  121.0 5.9 %fusion = f32[192,896]{1,0:T(8,128)} fusion(bf16[192,4096]{1,0:T(8,128)(2,1)S(1)} %bitcast.24, bf16[4096,1152]{1,0:T(8,128)(2,1)} %all-gather.3.cloned.1.call-done), kind=kOutput, calls=%fused_computation | convolution fusion | flops 1409286144 | bytes 9601024 | tf_op jit(solution)/shard_map/dot_general | solution.py:68
  126.9 1.2 all-gather.5.cloned.1.call-done
  128.0 5.9 %multiply_convert_fusion = (bf16[192,896]{1,0:T(8,128)(2,1)}, bf16[192,896]{1,0:T(8,128)(2,1)S(1)}, bf16[192,896]{1,0:T(8,128)(2,1)S(1)}) fusion(f32[192,896]{1,0:T(8,128)} %fusion, f32[192]{0:T(256)S(1)} %convert_reduce_fusion, bf16[192,896]{1,0:T(8,128)(2,1)S(1)} %copy-done.4, bf16[192,4096]{1,0:T(8,128)(2,1)S(1)} %bitcast.25, ...), kind=kOutput, calls=%fused_computation.19 | convolution fusion | flops 1412382720 | bytes 10978048 | tf_op jit(solution)/shard_map/dot_general | solution.py:69
  134.0 24.2 %all-to-all-done.4 = bf16[16,192,256]{2,1,0:T(8,128)(2,1)S(1)} async-done(((bf16[16,192,256]{2,1,0:T(8,128)(2,1)}), bf16[16,192,256]{2,1,0:T(8,128)(2,1)S(1)}, u32[]{:S(2)}, u32[]{:S(2)}) %all-to-all-start.4) | async-done | bytes 1572896 | tf_op jit(solution)/shard_map/all_to_all | solution.py:51
  158.2 5.3 %stack.2 = bf16[16,192,1792]{2,1,0:T(8,128)(2,1)} broadcast(bf16[192,1792]{1,0:T(8,128)(2,1)S(1)} %pad_maximum_fusion), dimensions={1,2} | broadcast | bytes 11698176 | tf_op jit(solution)/shard_map/stack | solution.py:80
  163.5 246.4 %all_to_all.36 = bf16[16,192,1792]{2,1,0:T(8,128)(2,1)S(1)} all-to-all(bf16[16,192,1792]{2,1,0:T(8,128)(2,1)} %stack.2), channel_id=1, replica_groups=mesh['dp'=16,'mp'=16] {'dp'}, dimensions={0} | all-to-all | bytes 22020096 | tf_op jit(solution)/shard_map/all_to_all | solution.py:80
  409.9 3.0 convolution_convert_fusion
  413.0 1.0 fusion.25
  (32 shorter events, 2.7 us)
Async XLA Ops:
  7.2 2.8 copy-start
  7.2 74.0 %all-gather.3.cloned.1.call-start = ((), (), s32[]{:S(2)}) async-start(), calls=%async_computation.6 | async-start | bytes 10027008 | tf_op jit(solution)/shard_map/all_gather | solution.py:28
  9.2 118.8 %all-gather.5.cloned.1.call-start = ((), (), s32[]{:S(2)}) async-start(), calls=%async_computation.7 | async-start | bytes 7798784 | tf_op jit(solution)/shard_map/all_gather | solution.py:30
  11.6 7.7 %copy-start.1 = (s32[16,192]{1,0:T(8,128)S(1)}, s32[16,192]{1,0:T(8,128)}, u32[]{:S(2)}) copy-start(s32[16,192]{1,0:T(8,128)} %param.13) | copy-start | bytes 36868
  11.6 7.7 %copy-start.2 = (s32[16]{0:T(128)S(1)}, s32[16]{0:T(128)}, u32[]{:S(2)}) copy-start(s32[16]{0:T(128)} %param.14) | copy-start | bytes 196
  11.6 38.7 %all-to-all-start = ((bf16[16,256,256]{1,2,0:T(8,128)(2,1)}), bf16[16,256,256]{1,2,0:T(8,128)(2,1)S(1)}, u32[]{:S(2)}, u32[]{:S(2)}) async-start(bf16[16,256,256]{1,2,0:T(8,128)(2,1)} %broadcast_in_dim.6), calls=%async_computation | async-start | bytes 4194304 | tf_op jit(solution)/shard_map/all_to_all | solution.py:9
  50.3 3.7 copy-start.3
  50.3 3.7 copy-start.5
  56.0 10.3 %all-to-all-start.1 = ((f32[16,1,256]{2,1,0:T(1,128)}), f32[16,1,256]{2,1,0:T(1,128)S(1)}, u32[]{:S(2)}, u32[]{:S(2)}) async-start(f32[16,1,256]{2,1,0:T(1,128)} %broadcast_in_dim.7), calls=%async_computation.1 | async-start | bytes 32768 | tf_op jit(solution)/shard_map/all_to_all | solution.py:9
  70.1 18.3 %all-to-all-start.2 = ((bf16[16,1,192]{2,1,0:T(2,128)(2,1)}), bf16[16,1,192]{2,1,0:T(2,128)(2,1)S(1)}, u32[]{:S(2)}, u32[]{:S(2)}) async-start(bf16[16,1,192]{2,1,0:T(2,128)(2,1)} %all_to_all.28), calls=%async_computation.2 | async-start | bytes 32768 | tf_op jit(solution)/shard_map/all_to_all | solution.py:66
  114.2 44.0 %all-to-all-start.4 = ((bf16[16,192,256]{2,1,0:T(8,128)(2,1)}), bf16[16,192,256]{2,1,0:T(8,128)(2,1)S(1)}, u32[]{:S(2)}, u32[]{:S(2)}) async-start(bf16[16,192,256]{2,1,0:T(8,128)(2,1)} %all_to_all.35), calls=%async_computation.4 | async-start | bytes 3145728 | tf_op jit(solution)/shard_map/all_to_all | solution.py:51
  120.9 7.1 %copy-start.4 = (bf16[192,896]{1,0:T(8,128)(2,1)S(1)}, bf16[192,896]{1,0:T(8,128)(2,1)}, u32[]{:S(2)}) copy-start(bf16[192,896]{1,0:T(8,128)(2,1)} %param.17) | copy-start | bytes 1032196
Sparse Core Ops, SparseCore 0:
  9.8 64.9 all-gather.2
  76.7 51.3 all-gather.4
